TPU v7x, 512 devices: a whole 4x4x16 slice. The times are simulated.
512 devices in a mesh: lon: 32 (over z, core), lat: 16 (over y, x).
Axes of the slice: x: 4, y: 4, z: 16, core: 2. Of those that a mesh axis runs over, the one named last changes fastest.
Arguments:
- perturbations: float32 [12, 3, 256, 4096], P(None, None, 'lat', 'lon'), as said below
- base_wind: float32 [2, 256, 4096], P(None, 'lat', 'lon'), may hold values from -4 to 4
- base_height: float32 [256, 4096], P('lat', 'lon'), may hold values from 0.5 to 1.5
Outputs:
- fields: float32 [12, 3, 256, 4096], P(None, None, 'lat', 'lon')
- factor: float32 [12, 12], replicated
Inputs may be any that keep to these rules, and one draw needn't show every extreme that they name: `perturbations`: finite real values.
All inputs are finite; a program needn't handle non-finite values.
Results may differ from a plain program's by a relative error of at most 0.00012.
Values sent between devices are 32-bit elements; how exact they have to be, the bound alone decides.
A program may use at most 64 MiB of HBM per device.

v0:
```python
import math
import jax
import jax.numpy as jnp
from jax import lax
from jax.sharding import PartitionSpec as P

STEPS = 8
advect_rate = 0.1
turn_rate = 0.5
gravity_rate = 0.2
diffuse_rate = 0.12


def with_halo(block, sides, width, periodic):
    for axis, dim in sides:
        count = lax.axis_size(axis)
        forward = [(i, i + 1) for i in range(count - 1)]
        if periodic:
            forward.append((count - 1, 0))
        backward = [(target, source) for source, target in forward]
        low = lax.ppermute(
            lax.slice_in_dim(block, block.shape[dim] - width, None, axis=dim), axis, forward
        )
        high = lax.ppermute(lax.slice_in_dim(block, 0, width, axis=dim), axis, backward)
        block = jnp.concatenate([low, block, high], axis=dim)
    return block


def centre(array):
    return array[..., 1:-1, 1:-1]


def diff_lon(array):
    return 0.5 * (array[..., 1:-1, 2:] - array[..., 1:-1, :-2])


def diff_lat(array):
    return 0.5 * (array[..., 2:, 1:-1] - array[..., :-2, 1:-1])


def laplacian(array):
    return (
        array[..., 2:, 1:-1]
        + array[..., :-2, 1:-1]
        + array[..., 1:-1, 2:]
        + array[..., 1:-1, :-2]
        - 4.0 * centre(array)
    )


def advance(field, base, turning):
    wind_x = field[..., 0, :, :]
    wind_y = field[..., 1, :, :]
    height = field[..., 2, :, :]
    base_x = base[0]
    base_y = base[1]
    base_depth = base[2]
    mean_x = centre(base_x)
    mean_y = centre(base_y)
    inner_x = centre(wind_x)
    inner_y = centre(wind_y)
    new_x = (
        inner_x
        - advect_rate
        * (
            mean_x * diff_lon(wind_x)
            + inner_x * diff_lon(base_x)
            + mean_y * diff_lat(wind_x)
            + inner_y * diff_lat(base_x)
        )
        + turn_rate * turning * inner_y
        - gravity_rate * diff_lon(height)
        + diffuse_rate * laplacian(wind_x)
    )
    new_y = (
        inner_y
        - advect_rate
        * (
            mean_x * diff_lon(wind_y)
            + inner_x * diff_lon(base_y)
            + mean_y * diff_lat(wind_y)
            + inner_y * diff_lat(base_y)
        )
        - turn_rate * turning * inner_x
        - gravity_rate * diff_lat(height)
        + diffuse_rate * laplacian(wind_y)
    )
    new_height = (
        centre(height)
        - advect_rate
        * (
            diff_lon(base_depth * wind_x + height * base_x)
            + diff_lat(base_depth * wind_y + height * base_y)
        )
        + diffuse_rate * laplacian(height)
    )
    return jnp.stack([new_x, new_y, new_height], axis=-3)


def coriolis(start, rows, total):
    glob = (start + jnp.arange(rows, dtype=jnp.int32)).astype(jnp.float32)
    return jnp.sin(math.pi * ((glob + 0.5) / total - 0.5))[:, None]


def inside_grid(start, rows, total):
    glob = start + jnp.arange(rows, dtype=jnp.int32)
    return ((glob >= 0) & (glob < total)).astype(jnp.float32)[:, None]


def extend(block, width):
    wide = with_halo(block, (("lon", 3),), width, True)
    return with_halo(wide, (("lat", 2),), width, False)


def per_device(perturbations, base_wind, base_height):
    rows = perturbations.shape[2]
    cols = perturbations.shape[3]
    total_rows = rows * lax.axis_size("lat")
    total_cols = cols * lax.axis_size("lon")
    row_start = lax.axis_index("lat") * rows
    depth = 2
    stacked = jnp.concatenate([base_wind, base_height[None]], axis=0)[None]
    base_ext = extend(stacked, depth)[0]
    field = perturbations
    for group_index in range(STEPS // depth):
        current = extend(field, depth)
        for inner_index in range(depth):
            margin = depth - 1 - inner_index
            turning = coriolis(row_start - margin, rows + 2 * margin, total_rows)
            base_margin = margin + 1
            current = advance(
                current,
                base_ext[
                    :,
                    depth - base_margin : depth + rows + base_margin,
                    depth - base_margin : depth + cols + base_margin,
                ],
                turning,
            )
            if margin > 0:
                current = current * inside_grid(row_start - margin, rows + 2 * margin, total_rows)
        field = current
    flattened = field.reshape(field.shape[0], -1)
    cell_count = float(3 * total_rows * total_cols)
    local_gram = jnp.dot(flattened, flattened.T, precision=lax.Precision.HIGHEST) / cell_count
    gram = lax.psum(local_gram, ("lon", "lat"))
    upper_factor = jnp.linalg.cholesky(gram).T
    lower_factor = upper_factor.T
    fields = jax.scipy.linalg.solve_triangular(lower_factor, flattened, lower=True)
    return (fields.reshape(perturbations.shape), upper_factor)


def solution(mesh):
    return jax.shard_map(
        per_device,
        mesh=mesh,
        in_specs=(P(None, None, "lat", "lon"), P(None, "lat", "lon"), P("lat", "lon")),
        out_specs=(P(None, None, "lat", "lon"), P()),
        check_vma=False,
    )
```

profile of v0, /device:TPU:1, one launch (start us, length us, event | category | flops | bytes accessed | tf_op | source)
XLA Modules:
  0.0 219.9 jit_solution(700765798616330664)
XLA Ops:
  0.6 0.7 maximum_bitcast_fusion
  1.4 3.0 %collective-permute-start.4 = (f32[1,3,16,2]{3,2,1,0:T(8,128)S(1)}, f32[1,3,16,2]{3,2,1,0:T(8,128)S(1)}, u32[]{:S(2)}, u32[]{:S(2)}) collective-permute-start(f32[1,3,16,2]{3,2,1,0:T(8,128)S(1)} %get-tuple-element.82), channel_id=1, source_target_pairs={{0,16},{16,32},{32,48},{48,64},{64,80},{80,96},{96,112},{112,128},... | collective-permute-start | bytes 1160 | tf_op jit(solution)/shard_map/ppermute | solution.py:21
  4.5 3.8 %collective-permute-start.5 = (f32[1,3,16,2]{3,2,1,0:T(8,128)S(1)}, f32[1,3,16,2]{3,2,1,0:T(8,128)S(1)}, u32[]{:S(2)}, u32[]{:S(2)}) collective-permute-start(f32[1,3,16,2]{3,2,1,0:T(8,128)S(1)} %get-tuple-element.83), channel_id=1, source_target_pairs={{16,0},{32,16},{48,32},{64,48},{80,64},{96,80},{112,96},{128,112},... | collective-permute-start | bytes 1160 | tf_op jit(solution)/shard_map/ppermute | solution.py:24
  8.3 1.1 copy.13
  9.6 3.6 %collective-permute-start.1 = (f32[12,3,16,2]{3,0,2,1:T(8,128)S(1)}, f32[12,3,16,2]{3,0,2,1:T(8,128)S(1)}, u32[]{:S(2)}, u32[]{:S(2)}) collective-permute-start(f32[12,3,16,2]{3,0,2,1:T(8,128)S(1)} %get-tuple-element.61), channel_id=1, source_target_pairs={{16,0},{32,16},{48,32},{64,48},{80,64},{96,80},{112,96},{128,112},... | collective-permute-start | bytes 13832 | tf_op jit(solution)/shard_map/ppermute | solution.py:24
  13.3 3.1 %collective-permute-start.6 = (f32[1,3,2,132]{3,2,1,0:T(2,128)S(1)}, f32[1,3,2,132]{3,2,1,0:T(2,128)S(1)}, u32[]{:S(2)}, u32[]{:S(2)}) collective-permute-start(f32[1,3,2,132]{3,2,1,0:T(2,128)S(1)} %get-tuple-element.68), channel_id=1, source_target_pairs={{0,1},{1,2},{2,3},{3,4},{4,5},{5,6},{6,7},{7,8},{8,9},{9,10},{10,1... | collective-permute-start | bytes 9512 | tf_op jit(solution)/shard_map/ppermute | solution.py:21
  16.5 1.3 collective-permute-start.7
  17.8 3.3 %collective-permute-done.7 = f32[1,3,2,132]{3,2,1,0:T(2,128)S(1)} collective-permute-done((f32[1,3,2,132]{3,2,1,0:T(2,128)S(1)}, f32[1,3,2,132]{3,2,1,0:T(2,128)S(1)}, u32[]{:S(2)}, u32[]{:S(2)}) %collective-permute-start.7) | collective-permute-done | bytes 3200 | tf_op jit(solution)/shard_map/ppermute | solution.py:24
  21.7 3.1 %collective-permute-start.2 = (f32[12,3,2,132]{3,0,2,1:T(8,128)S(1)}, f32[12,3,2,132]{3,0,2,1:T(8,128)S(1)}, u32[]{:S(2)}, u32[]{:S(2)}) collective-permute-start(f32[12,3,2,132]{3,0,2,1:T(8,128)S(1)} %get-tuple-element.12), channel_id=1, source_target_pairs={{0,1},{1,2},{2,3},{3,4},{4,5},{5,6},{6,7},{7,8},{8,9},{9,10},{10,1... | collective-permute-start | bytes 114056 | tf_op jit(solution)/shard_map/ppermute | solution.py:21
  24.9 1.3 collective-permute-start.3
  26.5 3.7 %collective-permute-done.3 = f32[12,3,2,132]{3,0,2,1:T(8,128)S(1)} collective-permute-done((f32[12,3,2,132]{3,0,2,1:T(8,128)S(1)}, f32[12,3,2,132]{3,0,2,1:T(8,128)S(1)}, u32[]{:S(2)}, u32[]{:S(2)}) %collective-permute-start.3) | collective-permute-done | bytes 38048 | tf_op jit(solution)/shard_map/ppermute | solution.py:24
  30.2 0.4 pad_maximum_fusion
  30.8 0.6 add_bitcast_fusion.7
  31.4 0.6 add_bitcast_fusion.6
  32.0 0.6 fusion.22
  33.3 0.3 add_bitcast_fusion.14
  33.6 0.3 fusion.42
  34.2 5.5 %collective-permute-start.9 = (f32[12,3,16,2]{3,0,2,1:T(8,128)S(1)}, f32[12,3,16,2]{3,0,2,1:T(8,128)S(1)}, u32[]{:S(2)}, u32[]{:S(2)}) collective-permute-start(f32[12,3,16,2]{3,0,2,1:T(8,128)S(1)} %get-tuple-element.59), channel_id=1, source_target_pairs={{16,0},{32,16},{48,32},{64,48},{80,64},{96,80},{112,96},{128,112},... | collective-permute-start | bytes 13832 | tf_op jit(solution)/shard_map/ppermute | solution.py:24
  39.7 1.2 collective-permute-done.8
  40.9 0.5 collective-permute-done.9
  41.5 4.7 %collective-permute-start.10 = (f32[12,3,2,132]{3,0,2,1:T(8,128)S(1)}, f32[12,3,2,132]{3,0,2,1:T(8,128)S(1)}, u32[]{:S(2)}, u32[]{:S(2)}) collective-permute-start(f32[12,3,2,132]{3,0,2,1:T(8,128)S(1)} %get-tuple-element.10), channel_id=1, source_target_pairs={{0,1},{1,2},{2,3},{3,4},{4,5},{5,6},{6,7},{7,8},{8,9},{9,10},{10,1... | collective-permute-start | bytes 114056 | tf_op jit(solution)/shard_map/ppermute | solution.py:21
  46.2 1.3 collective-permute-start.11
  47.5 0.3 collective-permute-done.10
  47.8 3.7 %collective-permute-done.11 = f32[12,3,2,132]{3,0,2,1:T(8,128)S(1)} collective-permute-done((f32[12,3,2,132]{3,0,2,1:T(8,128)S(1)}, f32[12,3,2,132]{3,0,2,1:T(8,128)S(1)}, u32[]{:S(2)}, u32[]{:S(2)}) %collective-permute-start.11) | collective-permute-done | bytes 38048 | tf_op jit(solution)/shard_map/ppermute | solution.py:24
  51.6 0.4 pad_maximum_fusion.1
  52.0 0.6 add_bitcast_fusion.5
  52.6 0.6 add_bitcast_fusion.4
  53.4 0.6 fusion.17
  54.5 0.3 add_bitcast_fusion.12
  55.0 0.3 fusion.37
  55.5 1.9 collective-permute-start.12
  57.4 6.0 %collective-permute-start.13 = (f32[12,3,16,2]{3,0,2,1:T(8,128)S(1)}, f32[12,3,16,2]{3,0,2,1:T(8,128)S(1)}, u32[]{:S(2)}, u32[]{:S(2)}) collective-permute-start(f32[12,3,16,2]{3,0,2,1:T(8,128)S(1)} %get-tuple-element.57), channel_id=1, source_target_pairs={{16,0},{32,16},{48,32},{64,48},{80,64},{96,80},{112,96},{128,112},... | collective-permute-start | bytes 13832 | tf_op jit(solution)/shard_map/ppermute | solution.py:24
  63.4 1.2 collective-permute-done.12
  64.9 3.8 %collective-permute-start.14 = (f32[12,3,2,132]{3,0,2,1:T(8,128)S(1)}, f32[12,3,2,132]{3,0,2,1:T(8,128)S(1)}, u32[]{:S(2)}, u32[]{:S(2)}) collective-permute-start(f32[12,3,2,132]{3,0,2,1:T(8,128)S(1)} %get-tuple-element.8), channel_id=1, source_target_pairs={{0,1},{1,2},{2,3},{3,4},{4,5},{5,6},{6,7},{7,8},{8,9},{9,10},{10,1... | collective-permute-start | bytes 114056 | tf_op jit(solution)/shard_map/ppermute | solution.py:21
  68.6 1.5 collective-permute-start.15
  70.2 4.0 %collective-permute-done.15 = f32[12,3,2,132]{3,0,2,1:T(8,128)S(1)} collective-permute-done((f32[12,3,2,132]{3,0,2,1:T(8,128)S(1)}, f32[12,3,2,132]{3,0,2,1:T(8,128)S(1)}, u32[]{:S(2)}, u32[]{:S(2)}) %collective-permute-start.15) | collective-permute-done | bytes 38048 | tf_op jit(solution)/shard_map/ppermute | solution.py:24
  74.3 0.4 pad_maximum_fusion.2
  74.7 0.6 add_bitcast_fusion.3
  75.3 0.6 add_bitcast_fusion.2
  76.1 0.6 fusion.12
  77.2 0.3 add_bitcast_fusion.10
  77.6 0.3 fusion.32
  78.2 1.0 collective-permute-start.16
  79.2 7.2 %collective-permute-start.17 = (f32[12,3,16,2]{3,0,2,1:T(8,128)S(1)}, f32[12,3,16,2]{3,0,2,1:T(8,128)S(1)}, u32[]{:S(2)}, u32[]{:S(2)}) collective-permute-start(f32[12,3,16,2]{3,0,2,1:T(8,128)S(1)} %get-tuple-element.55), channel_id=1, source_target_pairs={{16,0},{32,16},{48,32},{64,48},{80,64},{96,80},{112,96},{128,112},... | collective-permute-start | bytes 13832 | tf_op jit(solution)/shard_map/ppermute | solution.py:24
  86.4 1.2 collective-permute-done.16
  87.9 3.8 %collective-permute-start.18 = (f32[12,3,2,132]{3,0,2,1:T(8,128)S(1)}, f32[12,3,2,132]{3,0,2,1:T(8,128)S(1)}, u32[]{:S(2)}, u32[]{:S(2)}) collective-permute-start(f32[12,3,2,132]{3,0,2,1:T(8,128)S(1)} %get-tuple-element.6), channel_id=1, source_target_pairs={{0,1},{1,2},{2,3},{3,4},{4,5},{5,6},{6,7},{7,8},{8,9},{9,10},{10,1... | collective-permute-start | bytes 114056 | tf_op jit(solution)/shard_map/ppermute | solution.py:21
  91.7 1.3 collective-permute-start.19
  93.0 0.3 collective-permute-done.18
  93.3 4.0 %collective-permute-done.19 = f32[12,3,2,132]{3,0,2,1:T(8,128)S(1)} collective-permute-done((f32[12,3,2,132]{3,0,2,1:T(8,128)S(1)}, f32[12,3,2,132]{3,0,2,1:T(8,128)S(1)}, u32[]{:S(2)}, u32[]{:S(2)}) %collective-permute-start.19) | collective-permute-done | bytes 38048 | tf_op jit(solution)/shard_map/ppermute | solution.py:24
  97.3 0.4 pad_maximum_fusion.3
  97.7 0.6 add_bitcast_fusion.1
  98.3 0.6 add_bitcast_fusion
  99.1 0.6 fusion.7
  100.2 0.3 add_bitcast_fusion.8
  100.7 0.3 fusion.27
  101.0 0.6 fusion
  101.7 112.7 %psum.7 = f32[12,12]{0,1:T(8,128)S(1)} all-reduce(f32[12,12]{0,1:T(8,128)S(1)} %fusion), channel_id=1, replica_groups=mesh['lon'=32,'lat'=16] {'lon','lat'}, use_global_device_ids=true, to_apply=%region_0.0 | all-reduce | flops 144 | bytes 1152 | tf_op jit(solution)/shard_map/psum | solution.py:146
  214.4 1.1 cholesky.16
  215.5 0.6 compare_reduce_fusion
  216.2 0.6 fusion.53
  216.9 0.9 custom-call.7
  217.9 0.5 fusion.1
  218.4 0.8 copy.21
  219.2 0.7 copy.22
  (62 shorter events, 6.4 us)
Async XLA Ops:
  1.4 11.8 %collective-permute-start.4 = (f32[1,3,16,2]{3,2,1,0:T(8,128)S(1)}, f32[1,3,16,2]{3,2,1,0:T(8,128)S(1)}, u32[]{:S(2)}, u32[]{:S(2)}) collective-permute-start(f32[1,3,16,2]{3,2,1,0:T(8,128)S(1)} %get-tuple-element.82), channel_id=1, source_target_pairs={{0,16},{16,32},{32,48},{48,64},{64,80},{80,96},{96,112},{112,128},... | collective-permute-start | bytes 1160 | tf_op jit(solution)/shard_map/ppermute | solution.py:21
  4.5 8.8 %collective-permute-start.5 = (f32[1,3,16,2]{3,2,1,0:T(8,128)S(1)}, f32[1,3,16,2]{3,2,1,0:T(8,128)S(1)}, u32[]{:S(2)}, u32[]{:S(2)}) collective-permute-start(f32[1,3,16,2]{3,2,1,0:T(8,128)S(1)} %get-tuple-element.83), channel_id=1, source_target_pairs={{16,0},{32,16},{48,32},{64,48},{80,64},{96,80},{112,96},{128,112},... | collective-permute-start | bytes 1160 | tf_op jit(solution)/shard_map/ppermute | solution.py:24
  9.5 12.0 %collective-permute-start = (f32[12,3,16,2]{3,0,2,1:T(8,128)S(1)}, f32[12,3,16,2]{3,0,2,1:T(8,128)S(1)}, u32[]{:S(2)}, u32[]{:S(2)}) collective-permute-start(f32[12,3,16,2]{3,0,2,1:T(8,128)S(1)} %get-tuple-element.60), channel_id=1, source_target_pairs={{0,16},{16,32},{32,48},{48,64},{64,80},{80,96},{96,112},{112,128},... | collective-permute-start | bytes 13832 | tf_op jit(solution)/shard_map/ppermute | solution.py:21
  9.6 12.0 %collective-permute-start.1 = (f32[12,3,16,2]{3,0,2,1:T(8,128)S(1)}, f32[12,3,16,2]{3,0,2,1:T(8,128)S(1)}, u32[]{:S(2)}, u32[]{:S(2)}) collective-permute-start(f32[12,3,16,2]{3,0,2,1:T(8,128)S(1)} %get-tuple-element.61), channel_id=1, source_target_pairs={{16,0},{32,16},{48,32},{64,48},{80,64},{96,80},{112,96},{128,112},... | collective-permute-start | bytes 13832 | tf_op jit(solution)/shard_map/ppermute | solution.py:24
  13.3 4.5 %collective-permute-start.6 = (f32[1,3,2,132]{3,2,1,0:T(2,128)S(1)}, f32[1,3,2,132]{3,2,1,0:T(2,128)S(1)}, u32[]{:S(2)}, u32[]{:S(2)}) collective-permute-start(f32[1,3,2,132]{3,2,1,0:T(2,128)S(1)} %get-tuple-element.68), channel_id=1, source_target_pairs={{0,1},{1,2},{2,3},{3,4},{4,5},{5,6},{6,7},{7,8},{8,9},{9,10},{10,1... | collective-permute-start | bytes 9512 | tf_op jit(solution)/shard_map/ppermute | solution.py:21
  16.5 4.7 %collective-permute-start.7 = (f32[1,3,2,132]{3,2,1,0:T(2,128)S(1)}, f32[1,3,2,132]{3,2,1,0:T(2,128)S(1)}, u32[]{:S(2)}, u32[]{:S(2)}) collective-permute-start(f32[1,3,2,132]{3,2,1,0:T(2,128)S(1)} %get-tuple-element.69), channel_id=1, source_target_pairs={{1,0},{2,1},{3,2},{4,3},{5,4},{6,5},{7,6},{8,7},{9,8},{10,9},{11,1... | collective-permute-start | bytes 9512 | tf_op jit(solution)/shard_map/ppermute | solution.py:24
  21.7 4.7 %collective-permute-start.2 = (f32[12,3,2,132]{3,0,2,1:T(8,128)S(1)}, f32[12,3,2,132]{3,0,2,1:T(8,128)S(1)}, u32[]{:S(2)}, u32[]{:S(2)}) collective-permute-start(f32[12,3,2,132]{3,0,2,1:T(8,128)S(1)} %get-tuple-element.12), channel_id=1, source_target_pairs={{0,1},{1,2},{2,3},{3,4},{4,5},{5,6},{6,7},{7,8},{8,9},{9,10},{10,1... | collective-permute-start | bytes 114056 | tf_op jit(solution)/shard_map/ppermute | solution.py:21
  24.9 5.4 %collective-permute-start.3 = (f32[12,3,2,132]{3,0,2,1:T(8,128)S(1)}, f32[12,3,2,132]{3,0,2,1:T(8,128)S(1)}, u32[]{:S(2)}, u32[]{:S(2)}) collective-permute-start(f32[12,3,2,132]{3,0,2,1:T(8,128)S(1)} %get-tuple-element.13), channel_id=1, source_target_pairs={{1,0},{2,1},{3,2},{4,3},{5,4},{6,5},{7,6},{8,7},{9,8},{10,9},{11,1... | collective-permute-start | bytes 114056 | tf_op jit(solution)/shard_map/ppermute | solution.py:24
  34.1 6.7 %collective-permute-start.8 = (f32[12,3,16,2]{3,0,2,1:T(8,128)S(1)}, f32[12,3,16,2]{3,0,2,1:T(8,128)S(1)}, u32[]{:S(2)}, u32[]{:S(2)}) collective-permute-start(f32[12,3,16,2]{3,0,2,1:T(8,128)S(1)} %get-tuple-element.58), channel_id=1, source_target_pairs={{0,16},{16,32},{32,48},{48,64},{64,80},{80,96},{96,112},{112,128},... | collective-permute-start | bytes 13832 | tf_op jit(solution)/shard_map/ppermute | solution.py:21
  34.2 7.2 %collective-permute-start.9 = (f32[12,3,16,2]{3,0,2,1:T(8,128)S(1)}, f32[12,3,16,2]{3,0,2,1:T(8,128)S(1)}, u32[]{:S(2)}, u32[]{:S(2)}) collective-permute-start(f32[12,3,16,2]{3,0,2,1:T(8,128)S(1)} %get-tuple-element.59), channel_id=1, source_target_pairs={{16,0},{32,16},{48,32},{64,48},{80,64},{96,80},{112,96},{128,112},... | collective-permute-start | bytes 13832 | tf_op jit(solution)/shard_map/ppermute | solution.py:24
  41.5 6.3 %collective-permute-start.10 = (f32[12,3,2,132]{3,0,2,1:T(8,128)S(1)}, f32[12,3,2,132]{3,0,2,1:T(8,128)S(1)}, u32[]{:S(2)}, u32[]{:S(2)}) collective-permute-start(f32[12,3,2,132]{3,0,2,1:T(8,128)S(1)} %get-tuple-element.10), channel_id=1, source_target_pairs={{0,1},{1,2},{2,3},{3,4},{4,5},{5,6},{6,7},{7,8},{8,9},{9,10},{10,1... | collective-permute-start | bytes 114056 | tf_op jit(solution)/shard_map/ppermute | solution.py:21
  46.2 5.4 %collective-permute-start.11 = (f32[12,3,2,132]{3,0,2,1:T(8,128)S(1)}, f32[12,3,2,132]{3,0,2,1:T(8,128)S(1)}, u32[]{:S(2)}, u32[]{:S(2)}) collective-permute-start(f32[12,3,2,132]{3,0,2,1:T(8,128)S(1)} %get-tuple-element.11), channel_id=1, source_target_pairs={{1,0},{2,1},{3,2},{4,3},{5,4},{6,5},{7,6},{8,7},{9,8},{10,9},{11,1... | collective-permute-start | bytes 114056 | tf_op jit(solution)/shard_map/ppermute | solution.py:24
  55.5 9.1 %collective-permute-start.12 = (f32[12,3,16,2]{3,0,2,1:T(8,128)S(1)}, f32[12,3,16,2]{3,0,2,1:T(8,128)S(1)}, u32[]{:S(2)}, u32[]{:S(2)}) collective-permute-start(f32[12,3,16,2]{3,0,2,1:T(8,128)S(1)} %get-tuple-element.56), channel_id=1, source_target_pairs={{0,16},{16,32},{32,48},{48,64},{64,80},{80,96},{96,112},{112,128},... | collective-permute-start | bytes 13832 | tf_op jit(solution)/shard_map/ppermute | solution.py:21
  57.4 7.4 %collective-permute-start.13 = (f32[12,3,16,2]{3,0,2,1:T(8,128)S(1)}, f32[12,3,16,2]{3,0,2,1:T(8,128)S(1)}, u32[]{:S(2)}, u32[]{:S(2)}) collective-permute-start(f32[12,3,16,2]{3,0,2,1:T(8,128)S(1)} %get-tuple-element.57), channel_id=1, source_target_pairs={{16,0},{32,16},{48,32},{64,48},{80,64},{96,80},{112,96},{128,112},... | collective-permute-start | bytes 13832 | tf_op jit(solution)/shard_map/ppermute | solution.py:24
  64.9 5.4 %collective-permute-start.14 = (f32[12,3,2,132]{3,0,2,1:T(8,128)S(1)}, f32[12,3,2,132]{3,0,2,1:T(8,128)S(1)}, u32[]{:S(2)}, u32[]{:S(2)}) collective-permute-start(f32[12,3,2,132]{3,0,2,1:T(8,128)S(1)} %get-tuple-element.8), channel_id=1, source_target_pairs={{0,1},{1,2},{2,3},{3,4},{4,5},{5,6},{6,7},{7,8},{8,9},{9,10},{10,1... | collective-permute-start | bytes 114056 | tf_op jit(solution)/shard_map/ppermute | solution.py:21
  68.6 5.6 %collective-permute-start.15 = (f32[12,3,2,132]{3,0,2,1:T(8,128)S(1)}, f32[12,3,2,132]{3,0,2,1:T(8,128)S(1)}, u32[]{:S(2)}, u32[]{:S(2)}) collective-permute-start(f32[12,3,2,132]{3,0,2,1:T(8,128)S(1)} %get-tuple-element.9), channel_id=1, source_target_pairs={{1,0},{2,1},{3,2},{4,3},{5,4},{6,5},{7,6},{8,7},{9,8},{10,9},{11,1... | collective-permute-start | bytes 114056 | tf_op jit(solution)/shard_map/ppermute | solution.py:24
  78.2 9.4 %collective-permute-start.16 = (f32[12,3,16,2]{3,0,2,1:T(8,128)S(1)}, f32[12,3,16,2]{3,0,2,1:T(8,128)S(1)}, u32[]{:S(2)}, u32[]{:S(2)}) collective-permute-start(f32[12,3,16,2]{3,0,2,1:T(8,128)S(1)} %get-tuple-element.54), channel_id=1, source_target_pairs={{0,16},{16,32},{32,48},{48,64},{64,80},{80,96},{96,112},{112,128},... | collective-permute-start | bytes 13832 | tf_op jit(solution)/shard_map/ppermute | solution.py:21
  79.2 8.6 %collective-permute-start.17 = (f32[12,3,16,2]{3,0,2,1:T(8,128)S(1)}, f32[12,3,16,2]{3,0,2,1:T(8,128)S(1)}, u32[]{:S(2)}, u32[]{:S(2)}) collective-permute-start(f32[12,3,16,2]{3,0,2,1:T(8,128)S(1)} %get-tuple-element.55), channel_id=1, source_target_pairs={{16,0},{32,16},{48,32},{64,48},{80,64},{96,80},{112,96},{128,112},... | collective-permute-start | bytes 13832 | tf_op jit(solution)/shard_map/ppermute | solution.py:24
  87.9 5.4 %collective-permute-start.18 = (f32[12,3,2,132]{3,0,2,1:T(8,128)S(1)}, f32[12,3,2,132]{3,0,2,1:T(8,128)S(1)}, u32[]{:S(2)}, u32[]{:S(2)}) collective-permute-start(f32[12,3,2,132]{3,0,2,1:T(8,128)S(1)} %get-tuple-element.6), channel_id=1, source_target_pairs={{0,1},{1,2},{2,3},{3,4},{4,5},{5,6},{6,7},{7,8},{8,9},{9,10},{10,1... | collective-permute-start | bytes 114056 | tf_op jit(solution)/shard_map/ppermute | solution.py:21
  91.7 5.6 %collective-permute-start.19 = (f32[12,3,2,132]{3,0,2,1:T(8,128)S(1)}, f32[12,3,2,132]{3,0,2,1:T(8,128)S(1)}, u32[]{:S(2)}, u32[]{:S(2)}) collective-permute-start(f32[12,3,2,132]{3,0,2,1:T(8,128)S(1)} %get-tuple-element.7), channel_id=1, source_target_pairs={{1,0},{2,1},{3,2},{4,3},{5,4},{6,5},{7,6},{8,7},{9,8},{10,9},{11,1... | collective-permute-start | bytes 114056 | tf_op jit(solution)/shard_map/ppermute | solution.py:24
where the time goes:
time: 221 us; the launch traced here: 220 us
  blocking collectives  113 us (51%)
  starting transfers between devices  57.2 us (26%)
  waiting for transfers between devices  24.3 us (11%)
  other arithmetic  19.3 us (9%)
  local copies, waits for them, and re-layouts  4.13 us (2%)
    psum x1, blocking collectives, per_device(): gram = lax.psum(local_gram, ('lon', 'lat'))  113 us
    ppermute x10, starting transfers between devices, with_halo(): lax.ppermute(lax.slice_in_dim(block, 0, width, axis=dim), axis, backward)  32.8 us
    ppermute x10, starting transfers between devices, with_halo(): lax.ppermute(lax.slice_in_dim(block, block.shape[dim] - width, None, axis...  24.4 us
    ppermute x10, waiting for transfers between devices, with_halo(): lax.ppermute(lax.slice_in_dim(block, 0, width, axis=dim), axis, backward)  19.7 us
    another operation x28, other arithmetic, advance(): return jnp.stack([new_x, new_y, new_height], axis=-3)  11 us
    ppermute x10, waiting for transfers between devices, with_halo(): lax.ppermute(lax.slice_in_dim(block, block.shape[dim] - width, None, axis...  4.58 us
  transfers between devices with their start and end apart: 20, of which 15 were waited for; matrix products, arithmetic and copies ran while one was open for 1% of the time, Pallas kernels for 0%

commit v1 on v0

--- a/solution.py
+++ b/solution.py
@@ -143,7 +143,7 @@
     flattened = field.reshape(field.shape[0], -1)
     cell_count = float(3 * total_rows * total_cols)
     local_gram = jnp.dot(flattened, flattened.T, precision=lax.Precision.HIGHEST) / cell_count
-    gram = lax.psum(local_gram, ("lon", "lat"))
+    gram = jnp.sum(lax.all_gather(local_gram, ("lon", "lat")), axis=0)
     upper_factor = jnp.linalg.cholesky(gram).T
     lower_factor = upper_factor.T
     fields = jax.scipy.linalg.solve_triangular(lower_factor, flattened, lower=True)

time: 221 us -> 372 us (1.68)
  blocking collectives: 113 us -> 261 us
    all_gather x0 -> x1, blocking collectives: none -> 261 us  [per_device(): gram = jnp.sum(lax.all_gather(local_gram, ('lon', 'lat')), axis=0)]
    psum x1 -> x0, blocking collectives: 113 us -> none  [per_device(): gram = lax.psum(local_gram, ('lon', 'lat'))]
where the time goes in v1:
time: 372 us; the launch traced here: 371 us
  blocking collectives  261 us (70%)
  starting transfers between devices  57.2 us (15%)
  waiting for transfers between devices  24.3 us (7%)
  other arithmetic  22.1 us (6%)
  local copies, waits for them, and re-layouts  4.13 us (1%)
    all_gather x1, blocking collectives, per_device(): gram = jnp.sum(lax.all_gather(local_gram, ('lon', 'lat')), axis=0)  261 us
    ppermute x10, starting transfers between devices, with_halo(): lax.ppermute(lax.slice_in_dim(block, 0, width, axis=dim), axis, backward)  32.8 us
    ppermute x10, starting transfers between devices, with_halo(): lax.ppermute(lax.slice_in_dim(block, block.shape[dim] - width, None, axis...  24.4 us
    ppermute x10, waiting for transfers between devices, with_halo(): lax.ppermute(lax.slice_in_dim(block, 0, width, axis=dim), axis, backward)  19.7 us
    another operation x28, other arithmetic, advance(): return jnp.stack([new_x, new_y, new_height], axis=-3)  11 us
  transfers between devices with their start and end apart: 20, of which 15 were waited for; matrix products, arithmetic and copies ran while one was open for 1% of the time, Pallas kernels for 0%

profile of v1, /device:TPU:1, one launch (start us, length us, event | category | flops | bytes accessed | tf_op | source)
XLA Modules:
  0.0 371.2 jit_solution(12724543776136655561)
XLA Ops:
  0.6 0.7 maximum_bitcast_fusion
  1.4 3.0 collective-permute-start.4
  4.5 3.8 %collective-permute-start.5 = (f32[1,3,16,2]{3,2,1,0:T(8,128)S(1)}, f32[1,3,16,2]{3,2,1,0:T(8,128)S(1)}, u32[]{:S(2)}, u32[]{:S(2)}) collective-permute-start(f32[1,3,16,2]{3,2,1,0:T(8,128)S(1)} %get-tuple-element.85), channel_id=1, source_target_pairs={{16,0},{32,16},{48,32},{64,48},{80,64},{96,80},{112,96},{128,112},... | collective-permute-start | bytes 1160 | tf_op jit(solution)/shard_map/ppermute | solution.py:24
  8.3 1.1 copy.21
  9.6 3.6 collective-permute-start.1
  13.4 3.1 collective-permute-start.6
  16.5 1.3 collective-permute-start.7
  17.8 3.3 collective-permute-done.7
  21.7 3.1 collective-permute-start.2
  24.9 1.3 collective-permute-start.3
  26.5 3.7 %collective-permute-done.3 = f32[12,3,2,132]{3,0,2,1:T(8,128)S(1)} collective-permute-done((f32[12,3,2,132]{3,0,2,1:T(8,128)S(1)}, f32[12,3,2,132]{3,0,2,1:T(8,128)S(1)}, u32[]{:S(2)}, u32[]{:S(2)}) %collective-permute-start.3) | collective-permute-done | bytes 38048 | tf_op jit(solution)/shard_map/ppermute | solution.py:24
  30.2 0.4 pad_maximum_fusion
  30.8 0.6 fusion.23
  31.5 0.6 add_bitcast_fusion.7
  32.0 0.6 add_bitcast_fusion.6
  33.0 0.3 fusion.43
  33.6 0.3 add_bitcast_fusion.14
  34.2 5.5 %collective-permute-start.9 = (f32[12,3,16,2]{3,0,2,1:T(8,128)S(1)}, f32[12,3,16,2]{3,0,2,1:T(8,128)S(1)}, u32[]{:S(2)}, u32[]{:S(2)}) collective-permute-start(f32[12,3,16,2]{3,0,2,1:T(8,128)S(1)} %get-tuple-element.61), channel_id=1, source_target_pairs={{16,0},{32,16},{48,32},{64,48},{80,64},{96,80},{112,96},{128,112},... | collective-permute-start | bytes 13832 | tf_op jit(solution)/shard_map/ppermute | solution.py:24
  39.7 1.2 collective-permute-done.8
  40.9 0.5 collective-permute-done.9
  41.5 4.7 %collective-permute-start.10 = (f32[12,3,2,132]{3,0,2,1:T(8,128)S(1)}, f32[12,3,2,132]{3,0,2,1:T(8,128)S(1)}, u32[]{:S(2)}, u32[]{:S(2)}) collective-permute-start(f32[12,3,2,132]{3,0,2,1:T(8,128)S(1)} %get-tuple-element.12), channel_id=1, source_target_pairs={{0,1},{1,2},{2,3},{3,4},{4,5},{5,6},{6,7},{7,8},{8,9},{9,10},{10,1... | collective-permute-start | bytes 114056 | tf_op jit(solution)/shard_map/ppermute | solution.py:21
  46.3 1.3 collective-permute-start.11
  47.6 0.3 collective-permute-done.10
  47.9 3.7 %collective-permute-done.11 = f32[12,3,2,132]{3,0,2,1:T(8,128)S(1)} collective-permute-done((f32[12,3,2,132]{3,0,2,1:T(8,128)S(1)}, f32[12,3,2,132]{3,0,2,1:T(8,128)S(1)}, u32[]{:S(2)}, u32[]{:S(2)}) %collective-permute-start.11) | collective-permute-done | bytes 38048 | tf_op jit(solution)/shard_map/ppermute | solution.py:24
  51.6 0.4 pad_maximum_fusion.1
  52.2 0.6 add_bitcast_fusion.5
  52.8 0.6 add_bitcast_fusion.4
  53.4 0.6 fusion.18
  54.7 0.3 add_bitcast_fusion.12
  55.0 0.3 fusion.38
  55.5 1.9 collective-permute-start.12
  57.4 6.0 %collective-permute-start.13 = (f32[12,3,16,2]{3,0,2,1:T(8,128)S(1)}, f32[12,3,16,2]{3,0,2,1:T(8,128)S(1)}, u32[]{:S(2)}, u32[]{:S(2)}) collective-permute-start(f32[12,3,16,2]{3,0,2,1:T(8,128)S(1)} %get-tuple-element.59), channel_id=1, source_target_pairs={{16,0},{32,16},{48,32},{64,48},{80,64},{96,80},{112,96},{128,112},... | collective-permute-start | bytes 13832 | tf_op jit(solution)/shard_map/ppermute | solution.py:24
  63.4 1.2 collective-permute-done.12
  64.9 3.8 %collective-permute-start.14 = (f32[12,3,2,132]{3,0,2,1:T(8,128)S(1)}, f32[12,3,2,132]{3,0,2,1:T(8,128)S(1)}, u32[]{:S(2)}, u32[]{:S(2)}) collective-permute-start(f32[12,3,2,132]{3,0,2,1:T(8,128)S(1)} %get-tuple-element.10), channel_id=1, source_target_pairs={{0,1},{1,2},{2,3},{3,4},{4,5},{5,6},{6,7},{7,8},{8,9},{9,10},{10,1... | collective-permute-start | bytes 114056 | tf_op jit(solution)/shard_map/ppermute | solution.py:21
  68.7 1.5 collective-permute-start.15
  70.3 4.0 %collective-permute-done.15 = f32[12,3,2,132]{3,0,2,1:T(8,128)S(1)} collective-permute-done((f32[12,3,2,132]{3,0,2,1:T(8,128)S(1)}, f32[12,3,2,132]{3,0,2,1:T(8,128)S(1)}, u32[]{:S(2)}, u32[]{:S(2)}) %collective-permute-start.15) | collective-permute-done | bytes 38048 | tf_op jit(solution)/shard_map/ppermute | solution.py:24
  74.3 0.4 pad_maximum_fusion.2
  74.9 0.6 add_bitcast_fusion.3
  75.5 0.6 add_bitcast_fusion.2
  76.1 0.6 fusion.13
  77.3 0.3 add_bitcast_fusion.10
  77.7 0.3 fusion.33
  78.2 1.0 collective-permute-start.16
  79.2 7.2 %collective-permute-start.17 = (f32[12,3,16,2]{3,0,2,1:T(8,128)S(1)}, f32[12,3,16,2]{3,0,2,1:T(8,128)S(1)}, u32[]{:S(2)}, u32[]{:S(2)}) collective-permute-start(f32[12,3,16,2]{3,0,2,1:T(8,128)S(1)} %get-tuple-element.57), channel_id=1, source_target_pairs={{16,0},{32,16},{48,32},{64,48},{80,64},{96,80},{112,96},{128,112},... | collective-permute-start | bytes 13832 | tf_op jit(solution)/shard_map/ppermute | solution.py:24
  86.4 1.2 collective-permute-done.16
  87.9 3.8 %collective-permute-start.18 = (f32[12,3,2,132]{3,0,2,1:T(8,128)S(1)}, f32[12,3,2,132]{3,0,2,1:T(8,128)S(1)}, u32[]{:S(2)}, u32[]{:S(2)}) collective-permute-start(f32[12,3,2,132]{3,0,2,1:T(8,128)S(1)} %get-tuple-element.8), channel_id=1, source_target_pairs={{0,1},{1,2},{2,3},{3,4},{4,5},{5,6},{6,7},{7,8},{8,9},{9,10},{10,1... | collective-permute-start | bytes 114056 | tf_op jit(solution)/shard_map/ppermute | solution.py:21
  91.7 1.3 collective-permute-start.19
  93.0 0.3 collective-permute-done.18
  93.3 4.0 %collective-permute-done.19 = f32[12,3,2,132]{3,0,2,1:T(8,128)S(1)} collective-permute-done((f32[12,3,2,132]{3,0,2,1:T(8,128)S(1)}, f32[12,3,2,132]{3,0,2,1:T(8,128)S(1)}, u32[]{:S(2)}, u32[]{:S(2)}) %collective-permute-start.19) | collective-permute-done | bytes 38048 | tf_op jit(solution)/shard_map/ppermute | solution.py:24
  97.3 0.4 pad_maximum_fusion.3
  97.9 0.6 add_bitcast_fusion.1
  98.5 0.6 add_bitcast_fusion
  99.1 0.6 fusion.8
  100.4 0.3 add_bitcast_fusion.8
  101.0 0.6 fusion.1
  101.8 261.1 %all-gather.1 = f32[512,12,12]{2,1,0:T(8,128)} all-gather(f32[1,12,12]{2,1,0:T(8,128)S(1)} %fusion.1), channel_id=2, replica_groups=mesh['lon'=32,'lat'=16] {'lon','lat'}, dimensions={0}, use_global_device_ids=true | all-gather | bytes 295488 | tf_op jit(solution)/shard_map/all_gather | solution.py:146
  362.9 2.7 reduce_sum.9
  365.8 1.1 cholesky.16
  366.9 0.6 compare_reduce_fusion
  367.5 0.6 fusion.54
  368.2 0.7 copy.29
  368.9 0.9 custom-call.7
  369.8 0.6 fusion.2
  370.4 0.8 copy.28
  (63 shorter events, 6.7 us)
Async XLA Ops:
  1.4 11.8 %collective-permute-start.4 = (f32[1,3,16,2]{3,2,1,0:T(8,128)S(1)}, f32[1,3,16,2]{3,2,1,0:T(8,128)S(1)}, u32[]{:S(2)}, u32[]{:S(2)}) collective-permute-start(f32[1,3,16,2]{3,2,1,0:T(8,128)S(1)} %get-tuple-element.84), channel_id=1, source_target_pairs={{0,16},{16,32},{32,48},{48,64},{64,80},{80,96},{96,112},{112,128},... | collective-permute-start | bytes 1160 | tf_op jit(solution)/shard_map/ppermute | solution.py:21
  4.5 8.8 %collective-permute-start.5 = (f32[1,3,16,2]{3,2,1,0:T(8,128)S(1)}, f32[1,3,16,2]{3,2,1,0:T(8,128)S(1)}, u32[]{:S(2)}, u32[]{:S(2)}) collective-permute-start(f32[1,3,16,2]{3,2,1,0:T(8,128)S(1)} %get-tuple-element.85), channel_id=1, source_target_pairs={{16,0},{32,16},{48,32},{64,48},{80,64},{96,80},{112,96},{128,112},... | collective-permute-start | bytes 1160 | tf_op jit(solution)/shard_map/ppermute | solution.py:24
  9.5 12.1 %collective-permute-start = (f32[12,3,16,2]{3,0,2,1:T(8,128)S(1)}, f32[12,3,16,2]{3,0,2,1:T(8,128)S(1)}, u32[]{:S(2)}, u32[]{:S(2)}) collective-permute-start(f32[12,3,16,2]{3,0,2,1:T(8,128)S(1)} %get-tuple-element.62), channel_id=1, source_target_pairs={{0,16},{16,32},{32,48},{48,64},{64,80},{80,96},{96,112},{112,128},... | collective-permute-start | bytes 13832 | tf_op jit(solution)/shard_map/ppermute | solution.py:21
  9.6 12.0 %collective-permute-start.1 = (f32[12,3,16,2]{3,0,2,1:T(8,128)S(1)}, f32[12,3,16,2]{3,0,2,1:T(8,128)S(1)}, u32[]{:S(2)}, u32[]{:S(2)}) collective-permute-start(f32[12,3,16,2]{3,0,2,1:T(8,128)S(1)} %get-tuple-element.63), channel_id=1, source_target_pairs={{16,0},{32,16},{48,32},{64,48},{80,64},{96,80},{112,96},{128,112},... | collective-permute-start | bytes 13832 | tf_op jit(solution)/shard_map/ppermute | solution.py:24
  13.4 4.4 %collective-permute-start.6 = (f32[1,3,2,132]{3,2,1,0:T(2,128)S(1)}, f32[1,3,2,132]{3,2,1,0:T(2,128)S(1)}, u32[]{:S(2)}, u32[]{:S(2)}) collective-permute-start(f32[1,3,2,132]{3,2,1,0:T(2,128)S(1)} %get-tuple-element.70), channel_id=1, source_target_pairs={{0,1},{1,2},{2,3},{3,4},{4,5},{5,6},{6,7},{7,8},{8,9},{9,10},{10,1... | collective-permute-start | bytes 9512 | tf_op jit(solution)/shard_map/ppermute | solution.py:21
  16.5 4.7 %collective-permute-start.7 = (f32[1,3,2,132]{3,2,1,0:T(2,128)S(1)}, f32[1,3,2,132]{3,2,1,0:T(2,128)S(1)}, u32[]{:S(2)}, u32[]{:S(2)}) collective-permute-start(f32[1,3,2,132]{3,2,1,0:T(2,128)S(1)} %get-tuple-element.71), channel_id=1, source_target_pairs={{1,0},{2,1},{3,2},{4,3},{5,4},{6,5},{7,6},{8,7},{9,8},{10,9},{11,1... | collective-permute-start | bytes 9512 | tf_op jit(solution)/shard_map/ppermute | solution.py:24
  21.7 4.7 %collective-permute-start.2 = (f32[12,3,2,132]{3,0,2,1:T(8,128)S(1)}, f32[12,3,2,132]{3,0,2,1:T(8,128)S(1)}, u32[]{:S(2)}, u32[]{:S(2)}) collective-permute-start(f32[12,3,2,132]{3,0,2,1:T(8,128)S(1)} %get-tuple-element.14), channel_id=1, source_target_pairs={{0,1},{1,2},{2,3},{3,4},{4,5},{5,6},{6,7},{7,8},{8,9},{9,10},{10,1... | collective-permute-start | bytes 114056 | tf_op jit(solution)/shard_map/ppermute | solution.py:21
  24.9 5.4 %collective-permute-start.3 = (f32[12,3,2,132]{3,0,2,1:T(8,128)S(1)}, f32[12,3,2,132]{3,0,2,1:T(8,128)S(1)}, u32[]{:S(2)}, u32[]{:S(2)}) collective-permute-start(f32[12,3,2,132]{3,0,2,1:T(8,128)S(1)} %get-tuple-element.15), channel_id=1, source_target_pairs={{1,0},{2,1},{3,2},{4,3},{5,4},{6,5},{7,6},{8,7},{9,8},{10,9},{11,1... | collective-permute-start | bytes 114056 | tf_op jit(solution)/shard_map/ppermute | solution.py:24
  34.1 6.7 %collective-permute-start.8 = (f32[12,3,16,2]{3,0,2,1:T(8,128)S(1)}, f32[12,3,16,2]{3,0,2,1:T(8,128)S(1)}, u32[]{:S(2)}, u32[]{:S(2)}) collective-permute-start(f32[12,3,16,2]{3,0,2,1:T(8,128)S(1)} %get-tuple-element.60), channel_id=1, source_target_pairs={{0,16},{16,32},{32,48},{48,64},{64,80},{80,96},{96,112},{112,128},... | collective-permute-start | bytes 13832 | tf_op jit(solution)/shard_map/ppermute | solution.py:21
  34.2 7.2 %collective-permute-start.9 = (f32[12,3,16,2]{3,0,2,1:T(8,128)S(1)}, f32[12,3,16,2]{3,0,2,1:T(8,128)S(1)}, u32[]{:S(2)}, u32[]{:S(2)}) collective-permute-start(f32[12,3,16,2]{3,0,2,1:T(8,128)S(1)} %get-tuple-element.61), channel_id=1, source_target_pairs={{16,0},{32,16},{48,32},{64,48},{80,64},{96,80},{112,96},{128,112},... | collective-permute-start | bytes 13832 | tf_op jit(solution)/shard_map/ppermute | solution.py:24
  41.5 6.3 %collective-permute-start.10 = (f32[12,3,2,132]{3,0,2,1:T(8,128)S(1)}, f32[12,3,2,132]{3,0,2,1:T(8,128)S(1)}, u32[]{:S(2)}, u32[]{:S(2)}) collective-permute-start(f32[12,3,2,132]{3,0,2,1:T(8,128)S(1)} %get-tuple-element.12), channel_id=1, source_target_pairs={{0,1},{1,2},{2,3},{3,4},{4,5},{5,6},{6,7},{7,8},{8,9},{9,10},{10,1... | collective-permute-start | bytes 114056 | tf_op jit(solution)/shard_map/ppermute | solution.py:21
  46.3 5.4 %collective-permute-start.11 = (f32[12,3,2,132]{3,0,2,1:T(8,128)S(1)}, f32[12,3,2,132]{3,0,2,1:T(8,128)S(1)}, u32[]{:S(2)}, u32[]{:S(2)}) collective-permute-start(f32[12,3,2,132]{3,0,2,1:T(8,128)S(1)} %get-tuple-element.13), channel_id=1, source_target_pairs={{1,0},{2,1},{3,2},{4,3},{5,4},{6,5},{7,6},{8,7},{9,8},{10,9},{11,1... | collective-permute-start | bytes 114056 | tf_op jit(solution)/shard_map/ppermute | solution.py:24
  55.5 9.1 %collective-permute-start.12 = (f32[12,3,16,2]{3,0,2,1:T(8,128)S(1)}, f32[12,3,16,2]{3,0,2,1:T(8,128)S(1)}, u32[]{:S(2)}, u32[]{:S(2)}) collective-permute-start(f32[12,3,16,2]{3,0,2,1:T(8,128)S(1)} %get-tuple-element.58), channel_id=1, source_target_pairs={{0,16},{16,32},{32,48},{48,64},{64,80},{80,96},{96,112},{112,128},... | collective-permute-start | bytes 13832 | tf_op jit(solution)/shard_map/ppermute | solution.py:21
  57.4 7.4 %collective-permute-start.13 = (f32[12,3,16,2]{3,0,2,1:T(8,128)S(1)}, f32[12,3,16,2]{3,0,2,1:T(8,128)S(1)}, u32[]{:S(2)}, u32[]{:S(2)}) collective-permute-start(f32[12,3,16,2]{3,0,2,1:T(8,128)S(1)} %get-tuple-element.59), channel_id=1, source_target_pairs={{16,0},{32,16},{48,32},{64,48},{80,64},{96,80},{112,96},{128,112},... | collective-permute-start | bytes 13832 | tf_op jit(solution)/shard_map/ppermute | solution.py:24
  64.9 5.4 %collective-permute-start.14 = (f32[12,3,2,132]{3,0,2,1:T(8,128)S(1)}, f32[12,3,2,132]{3,0,2,1:T(8,128)S(1)}, u32[]{:S(2)}, u32[]{:S(2)}) collective-permute-start(f32[12,3,2,132]{3,0,2,1:T(8,128)S(1)} %get-tuple-element.10), channel_id=1, source_target_pairs={{0,1},{1,2},{2,3},{3,4},{4,5},{5,6},{6,7},{7,8},{8,9},{9,10},{10,1... | collective-permute-start | bytes 114056 | tf_op jit(solution)/shard_map/ppermute | solution.py:21
  68.7 5.6 %collective-permute-start.15 = (f32[12,3,2,132]{3,0,2,1:T(8,128)S(1)}, f32[12,3,2,132]{3,0,2,1:T(8,128)S(1)}, u32[]{:S(2)}, u32[]{:S(2)}) collective-permute-start(f32[12,3,2,132]{3,0,2,1:T(8,128)S(1)} %get-tuple-element.11), channel_id=1, source_target_pairs={{1,0},{2,1},{3,2},{4,3},{5,4},{6,5},{7,6},{8,7},{9,8},{10,9},{11,1... | collective-permute-start | bytes 114056 | tf_op jit(solution)/shard_map/ppermute | solution.py:24
  78.2 9.4 %collective-permute-start.16 = (f32[12,3,16,2]{3,0,2,1:T(8,128)S(1)}, f32[12,3,16,2]{3,0,2,1:T(8,128)S(1)}, u32[]{:S(2)}, u32[]{:S(2)}) collective-permute-start(f32[12,3,16,2]{3,0,2,1:T(8,128)S(1)} %get-tuple-element.56), channel_id=1, source_target_pairs={{0,16},{16,32},{32,48},{48,64},{64,80},{80,96},{96,112},{112,128},... | collective-permute-start | bytes 13832 | tf_op jit(solution)/shard_map/ppermute | solution.py:21
  79.2 8.6 %collective-permute-start.17 = (f32[12,3,16,2]{3,0,2,1:T(8,128)S(1)}, f32[12,3,16,2]{3,0,2,1:T(8,128)S(1)}, u32[]{:S(2)}, u32[]{:S(2)}) collective-permute-start(f32[12,3,16,2]{3,0,2,1:T(8,128)S(1)} %get-tuple-element.57), channel_id=1, source_target_pairs={{16,0},{32,16},{48,32},{64,48},{80,64},{96,80},{112,96},{128,112},... | collective-permute-start | bytes 13832 | tf_op jit(solution)/shard_map/ppermute | solution.py:24
  87.9 5.4 %collective-permute-start.18 = (f32[12,3,2,132]{3,0,2,1:T(8,128)S(1)}, f32[12,3,2,132]{3,0,2,1:T(8,128)S(1)}, u32[]{:S(2)}, u32[]{:S(2)}) collective-permute-start(f32[12,3,2,132]{3,0,2,1:T(8,128)S(1)} %get-tuple-element.8), channel_id=1, source_target_pairs={{0,1},{1,2},{2,3},{3,4},{4,5},{5,6},{6,7},{7,8},{8,9},{9,10},{10,1... | collective-permute-start | bytes 114056 | tf_op jit(solution)/shard_map/ppermute | solution.py:21
  91.7 5.6 %collective-permute-start.19 = (f32[12,3,2,132]{3,0,2,1:T(8,128)S(1)}, f32[12,3,2,132]{3,0,2,1:T(8,128)S(1)}, u32[]{:S(2)}, u32[]{:S(2)}) collective-permute-start(f32[12,3,2,132]{3,0,2,1:T(8,128)S(1)} %get-tuple-element.9), channel_id=1, source_target_pairs={{1,0},{2,1},{3,2},{4,3},{5,4},{6,5},{7,6},{8,7},{9,8},{10,9},{11,1... | collective-permute-start | bytes 114056 | tf_op jit(solution)/shard_map/ppermute | solution.py:24
